TPU v7x, 256 devices: a whole 4x4x8 slice. The times are simulated.
256 devices in a mesh: row: 32 (over y, z_lo, core), col: 8 (over x, z_hi).
Axes of the slice: x: 4, y: 4, z: 8 (z_hi: 2, z_lo: 4; z = z_hi * 4 + z_lo), core: 2. Of those that a mesh axis runs over, the one named last changes fastest.
Arguments:
- frames: bfloat16 [256, 3, 12288], P('col', None, 'row'), may hold values from -6 to 6
- rotations: float32 [3, 3, 256], replicated, may hold values from -1 to 1, as said below
- inverse_cov: float32 [12288, 12288], P('row', 'col'), may hold values from -1 to 11, as said below
Outputs:
- covariance: float32 [12288, 12288], P('row', 'col')
- fitted_rotations: float32 [3, 3, 256], P(None, None, 'col')
Inputs may be any that keep to these rules, and one draw needn't show every extreme that they name: `rotations`: each frame's 3 x 3 matrix is a rotation. `inverse_cov`: symmetric.
All inputs are finite; a program needn't handle non-finite values.
Results may differ from a plain program's by a relative error of at most 0.00031.
Values may be sent and summed in bfloat16 or wider, within the bound.
A program may use at most 64 MiB of HBM per device.

v0:
```python
import jax
import jax.numpy as jnp
from jax import lax
from jax.sharding import PartitionSpec as P

POLAR = 12


def orthogonalize(fitted):
    scaling = jnp.sqrt(1.0 + jnp.sum(fitted * fitted, axis=(0, 1)))
    current = jnp.transpose(fitted, (1, 0, 2)) / scaling
    for sweep in range(POLAR):
        square = jnp.einsum("ijf,kjf->ikf", current, current, precision=lax.Precision.HIGHEST)
        cubed_term = jnp.einsum("ikf,klf->ilf", square, current, precision=lax.Precision.HIGHEST)
        current = 1.5 * current - 0.5 * cubed_term
    return current


def deviations_of(transforms, coords_half, centre_block):
    moved = jnp.einsum(
        "klf,fla->fka", transforms, coords_half.astype(jnp.float32), precision=lax.Precision.HIGHEST
    )
    values = (moved - centre_block[None]).astype(jnp.bfloat16)
    return values.reshape(values.shape[0] * 3, values.shape[2])


def tile_block(rows_operand, column_panel):
    return lax.dot_general(
        rows_operand, column_panel, (((0,), (0,)), ((), ())), preferred_element_type=jnp.float32
    )


def per_device(frames, rotations, inverse_cov):
    col_width = inverse_cov.shape[1]
    col_count = lax.axis_size("col")
    col_index = lax.axis_index("col")
    frame_total = frames.shape[0] * col_count
    offset = col_index * frames.shape[0]
    local_rot = lax.dynamic_slice_in_dim(rotations, offset, frames.shape[0], 2)
    coords = frames.astype(jnp.float32)
    partial_value = jnp.einsum("klf,fla->ka", local_rot, coords, precision=lax.Precision.HIGHEST)
    centre_rows = lax.psum(partial_value, "col") / frame_total
    centre_all = lax.all_gather(centre_rows, "row", axis=1, tiled=True)
    centre_cols = lax.dynamic_slice_in_dim(centre_all, col_index * col_width, col_width, 1)
    local_weight = lax.dot_general(
        centre_cols, inverse_cov, (((1,), (1,)), ((), ())), precision=lax.Precision.HIGHEST
    )
    weighted = lax.psum(local_weight, "col")
    fit_part = jnp.einsum("fka,la->klf", coords, weighted, precision=lax.Precision.HIGHEST)
    fitted = lax.psum(fit_part, "row")
    transforms = orthogonalize(fitted)
    local_dev = deviations_of(transforms, frames, centre_rows)
    rows_operand = lax.all_gather(local_dev, "col", axis=0, tiled=True)
    dev_atoms = lax.all_gather(local_dev, "row", axis=1, tiled=True)
    column_panel = lax.all_to_all(dev_atoms, "col", split_axis=1, concat_axis=0, tiled=True)
    covariance = tile_block(rows_operand, column_panel) / (3 * frame_total)
    return (covariance, transforms)


def solution(mesh):
    placed = (P("col", None, "row"), P(), P("row", "col"))
    return jax.shard_map(
        per_device,
        mesh=mesh,
        in_specs=placed,
        out_specs=(P("row", "col"), P(None, None, "col")),
        check_vma=False,
    )
```

profile of v0, /device:TPU:40, one launch (start us, length us, event | category | flops | bytes accessed | tf_op | source)
XLA Modules:
  0.0 377.9 jit_solution(10751000671556221047)
XLA Ops:
  7.2 0.9 constant_dynamic-slice_fusion
  8.2 1.1 convolution_bitcast_fusion.13
  9.3 32.8 %psum.21 = f32[3,384]{1,0:T(4,128)S(1)} all-reduce(f32[3,384]{1,0:T(4,128)S(1)} %convolution_bitcast_fusion.13), channel_id=1, replica_groups=mesh['row'=32,'col'=8] {'col'}, use_global_device_ids=true, to_apply=%region_0.0 | all-reduce | flops 1152 | bytes 9216 | tf_op jit(solution)/shard_map/psum | solution.py:42
  42.1 34.4 %all_gather.9 = f32[3,12288]{1,0:T(4,128)S(1)} all-gather(f32[3,384]{1,0:T(4,128)S(1)} %broadcast_multiply_fusion), channel_id=1, replica_groups=mesh['row'=32,'col'=8] {'row'}, dimensions={1}, use_global_device_ids=true | all-gather | bytes 152064 | tf_op jit(solution)/shard_map/all_gather | solution.py:43
  76.5 2.0 fusion.2
  78.5 24.2 %psum.22 = f32[3,384]{1,0:T(4,128)S(1)} all-reduce(f32[3,384]{1,0:T(4,128)S(1)} %fusion.2), channel_id=1, replica_groups=mesh['row'=32,'col'=8] {'col'}, use_global_device_ids=true, to_apply=%region_1.0 | all-reduce | flops 1152 | bytes 9216 | tf_op jit(solution)/shard_map/psum | solution.py:48
  102.7 0.2 convolution_bitcast_fusion.12
  102.9 56.1 %psum.23 = f32[3,3,32]{2,1,0:T(4,128)S(1)} all-reduce(f32[3,3,32]{2,1,0:T(4,128)S(1)} %convolution_bitcast_fusion.12), channel_id=1, replica_groups=mesh['row'=32,'col'=8] {'row'}, use_global_device_ids=true, to_apply=%region_2.0 | all-reduce | flops 288 | bytes 2304 | tf_op jit(solution)/shard_map/psum | solution.py:50
  159.0 0.1 copy.36
  159.2 0.4 convolution_bitcast_fusion.11
  159.6 0.3 fusion.7
  159.9 0.1 copy.37
  160.1 0.1 copy.38
  160.2 0.4 convolution_bitcast_fusion.10
  160.6 0.3 fusion.8
  161.0 0.1 copy.39
  161.1 0.1 copy.40
  161.2 0.4 convolution_bitcast_fusion.9
  161.6 0.3 fusion.9
  162.0 0.1 copy.41
  162.1 0.1 copy.42
  162.2 0.4 convolution_bitcast_fusion.8
  162.6 0.3 fusion.10
  163.0 0.1 copy.43
  163.1 0.1 copy.44
  163.2 0.4 convolution_bitcast_fusion.7
  163.6 0.3 fusion.11
  164.0 0.1 copy.45
  164.1 0.1 copy.46
  164.2 0.4 convolution_bitcast_fusion.6
  164.7 0.3 fusion.12
  165.0 0.1 copy.47
  165.1 0.1 copy.48
  165.2 0.4 convolution_bitcast_fusion.5
  165.7 0.3 fusion.13
  166.0 0.1 copy.49
  166.1 0.1 copy.50
  166.2 0.4 convolution_bitcast_fusion.4
  166.7 0.3 fusion.14
  167.0 0.1 copy.51
  167.1 0.1 copy.52
  167.2 0.4 convolution_bitcast_fusion.3
  167.7 0.3 fusion.15
  168.0 0.1 copy.53
  168.1 0.1 copy.54
  168.3 0.4 convolution_bitcast_fusion.2
  168.7 0.3 fusion.16
  169.1 0.1 copy.56
  169.3 0.4 convolution_bitcast_fusion.1
  169.7 0.3 fusion.17
  170.0 0.1 copy.57
  170.1 0.1 copy.58
  170.3 0.4 convolution_bitcast_fusion
  170.7 0.3 fusion.18
  171.1 0.1 copy.59
  171.2 0.1 copy.60
  171.3 0.4 fusion
  171.6 0.7 reshape.15
  172.4 77.7 %all-gather.2.cloned.1.call-done = bf16[96,12288]{1,0:T(8,128)(2,1)} async-done(((bf16[96,384]{1,0:T(8,128)(2,1)}), bf16[96,12288]{1,0:T(8,128)(2,1)}) %all-gather.2.cloned.1.call-update) | async-done | bytes 2359312 | tf_op jit(solution)/shard_map/all_gather | solution.py:54
  250.1 3.3 copy.83
  253.4 8.1 %all-to-all-start = ((bf16[96,8,1536]{2,0,1:T(8,128)(2,1)}), bf16[96,8,1536]{2,0,1:T(8,128)(2,1)}, u32[]{:S(2)}, u32[]{:S(2)}) async-start(bf16[96,8,1536]{2,0,1:T(8,128)(2,1)} %bitcast.118), calls=%async_computation | async-start | bytes 4718592 | tf_op jit(solution)/shard_map/all_to_all | solution.py:55
  261.5 0.6 copy.63
  262.1 104.9 %all_gather.10 = bf16[768,384]{1,0:T(8,128)(2,1)S(1)} all-gather(bf16[96,384]{1,0:T(8,128)(2,1)S(1)} %copy-done.1), channel_id=1, replica_groups=mesh['row'=32,'col'=8] {'col'}, dimensions={0}, use_global_device_ids=true | all-gather | bytes 663552 | tf_op jit(solution)/shard_map/all_gather | solution.py:53
  366.9 4.2 %convolution_multiply_fusion = f32[384,1536]{1,0:T(8,128)} fusion(bf16[768,384]{1,0:T(8,128)(2,1)S(1)} %all_gather.10, bf16[768,1536]{1,0:T(8,128)(2,1)} %bitcast.29), kind=kOutput, calls=%fused_computation | convolution fusion | flops 906559488 | bytes 5308416 | tf_op jit(solution)/shard_map/dot_general | solution.py:28
  (26 shorter events, 0.3 us)
Async XLA Ops:
  7.2 69.3 %copy-start = (f32[384,1536]{1,0:T(8,128)S(1)}, f32[384,1536]{1,0:T(8,128)}, u32[]{:S(2)}) copy-start(f32[384,1536]{1,0:T(8,128)} %param.5) | copy-start | bytes 7077892
  7.2 95.5 %copy-start.2 = (bf16[32,3,384]{2,0,1:T(8,128)(2,1)S(1)}, bf16[32,3,384]{2,0,1:T(8,128)(2,1)}, u32[]{:S(2)}) copy-start(bf16[32,3,384]{2,0,1:T(8,128)(2,1)} %param.3) | copy-start | bytes 221188
  7.2 242.9 %all-gather.2.cloned.1.call-start = ((), (), s32[]{:S(2)}) async-start(), calls=%async_computation.1 | async-start | bytes 2433024 | tf_op jit(solution)/shard_map/all_gather | solution.py:54
  253.4 8.7 %copy-start.1 = (bf16[96,384]{1,0:T(8,128)(2,1)S(1)}, bf16[96,384]{1,0:T(8,128)(2,1)}, u32[]{:S(2)}) copy-start(bf16[96,384]{1,0:T(8,128)(2,1)} %reshape.15) | copy-start | bytes 221188
  253.4 113.6 %all-to-all-start = ((bf16[96,8,1536]{2,0,1:T(8,128)(2,1)}), bf16[96,8,1536]{2,0,1:T(8,128)(2,1)}, u32[]{:S(2)}, u32[]{:S(2)}) async-start(bf16[96,8,1536]{2,0,1:T(8,128)(2,1)} %bitcast.118), calls=%async_computation | async-start | bytes 4718592 | tf_op jit(solution)/shard_map/all_to_all | solution.py:55
Sparse Core Ops, SparseCore 0:
  172.5 77.5 all-gather.1
where the time goes:
time: 378 us
  blocking collectives  252 us (67%)
  waiting for transfers between devices  77.7 us (21%)
  matrix products  17.1 us (5%)
  between operations  14.4 us (4%)
  starting transfers between devices  8.13 us (2%)
  local copies, waits for them, and re-layouts  8.1 us (2%)
    all_gather x1, blocking collectives, per_device(): rows_operand = lax.all_gather(local_dev, 'col', axis=0, tiled=True)  105 us
    all_gather x1, waiting for transfers between devices, per_device(): dev_atoms = lax.all_gather(local_dev, 'row', axis=1, tiled=True)  77.7 us
    psum x1, blocking collectives, per_device(): fitted = lax.psum(fit_part, 'row')  56.1 us
    all_gather x1, blocking collectives, per_device(): centre_all = lax.all_gather(centre_rows, 'row', axis=1, tiled=True)  34.4 us
    psum x1, blocking collectives, per_device(): centre_rows = lax.psum(partial_value, 'col') / frame_total  32.8 us
    psum x1, blocking collectives, per_device(): weighted = lax.psum(local_weight, 'col')  24.2 us
    all_to_all x1, starting transfers between devices, per_device(): lax.all_to_all(dev_atoms, 'col', split_axis=1, concat_axis=0, tiled=True)  8.09 us
  transfers between devices with their start and end apart: 2, of which 1 were waited for; matrix products, arithmetic and copies ran while one was open for 0% of the time, Pallas kernels for 0%

commit v1 on v0

--- a/solution.py
+++ b/solution.py
@@ -47,7 +47,7 @@
     )
     weighted = lax.psum(local_weight, "col")
     fit_part = jnp.einsum("fka,la->klf", coords, weighted, precision=lax.Precision.HIGHEST)
-    fitted = lax.psum(fit_part, "row")
+    fitted = jnp.sum(lax.all_gather(fit_part, "row"), axis=0)
     transforms = orthogonalize(fitted)
     local_dev = deviations_of(transforms, frames, centre_rows)
     rows_operand = lax.all_gather(local_dev, "col", axis=0, tiled=True)

time: 378 us -> 349 us (0.923); the launches traced: 378 us -> 344 us
  blocking collectives: 252 us -> 232 us
  waiting for transfers between devices: 77.7 us -> 63.8 us
    psum x1 -> x0, blocking collectives: 56.1 us -> none  [per_device(): fitted = lax.psum(fit_part, 'row')]
    all_gather x0 -> x1, blocking collectives: none -> 40.6 us  [per_device(): fitted = jnp.sum(lax.all_gather(fit_part, 'row'), axis=0)]
    all_gather x1, waiting for transfers between devices: 77.7 us -> 63.8 us  [per_device(): dev_atoms = lax.all_gather(local_dev, 'row', axis=1, tiled=True)]
    all_gather x1, blocking collectives: 105 us -> 100 us  [per_device(): rows_operand = lax.all_gather(local_dev, 'col', axis=0, tiled=True)]
where the time goes in v1:
time: 349 us; the launch traced here: 344 us
  blocking collectives  232 us (66%)
  waiting for transfers between devices  63.8 us (18%)
  matrix products  17.3 us (5%)
  between operations  14.4 us (4%)
  starting transfers between devices  8.23 us (2%)
  local copies, waits for them, and re-layouts  8.11 us (2%)
    all_gather x1, blocking collectives, per_device(): rows_operand = lax.all_gather(local_dev, 'col', axis=0, tiled=True)  100 us
    all_gather x1, waiting for transfers between devices, per_device(): dev_atoms = lax.all_gather(local_dev, 'row', axis=1, tiled=True)  63.8 us
    all_gather x1, blocking collectives, per_device(): fitted = jnp.sum(lax.all_gather(fit_part, 'row'), axis=0)  40.6 us
    all_gather x1, blocking collectives, per_device(): centre_all = lax.all_gather(centre_rows, 'row', axis=1, tiled=True)  34.4 us
    psum x1, blocking collectives, per_device(): centre_rows = lax.psum(partial_value, 'col') / frame_total  32.8 us
    psum x1, blocking collectives, per_device(): weighted = lax.psum(local_weight, 'col')  24.2 us
    all_to_all x1, starting transfers between devices, per_device(): lax.all_to_all(dev_atoms, 'col', split_axis=1, concat_axis=0, tiled=True)  8.2 us
  transfers between devices with their start and end apart: 2, of which 1 were waited for; matrix products, arithmetic and copies ran while one was open for 0% of the time, Pallas kernels for 0%

profile of v1, /device:TPU:40, one launch (start us, length us, event | category | flops | bytes accessed | tf_op | source)
XLA Modules:
  0.0 344.2 jit_solution(9709880324835737811)
XLA Ops:
  7.2 0.9 constant_dynamic-slice_fusion
  8.2 1.1 convolution_bitcast_fusion.13
  9.3 32.8 %psum.14 = f32[3,384]{1,0:T(4,128)S(1)} all-reduce(f32[3,384]{1,0:T(4,128)S(1)} %convolution_bitcast_fusion.13), channel_id=1, replica_groups=mesh['row'=32,'col'=8] {'col'}, use_global_device_ids=true, to_apply=%region_0.0 | all-reduce | flops 1152 | bytes 9216 | tf_op jit(solution)/shard_map/psum | solution.py:42
  42.1 34.4 %all_gather.15 = f32[3,12288]{1,0:T(4,128)S(1)} all-gather(f32[3,384]{1,0:T(4,128)S(1)} %broadcast_multiply_fusion), channel_id=1, replica_groups=mesh['row'=32,'col'=8] {'row'}, dimensions={1}, use_global_device_ids=true | all-gather | bytes 152064 | tf_op jit(solution)/shard_map/all_gather | solution.py:43
  76.5 2.0 fusion.2
  78.5 24.2 %psum.15 = f32[3,384]{1,0:T(4,128)S(1)} all-reduce(f32[3,384]{1,0:T(4,128)S(1)} %fusion.2), channel_id=1, replica_groups=mesh['row'=32,'col'=8] {'col'}, use_global_device_ids=true, to_apply=%region_1.0 | all-reduce | flops 1152 | bytes 9216 | tf_op jit(solution)/shard_map/psum | solution.py:48
  102.7 0.2 convolution_bitcast_fusion.12
  102.9 40.6 %all-gather = f32[96,3,32]{2,1,0:T(4,128)S(1)} all-gather(f32[3,3,32]{2,1,0:T(4,128)S(1)} %convolution_bitcast_fusion.12), channel_id=2, replica_groups=mesh['row'=32,'col'=8] {'row'}, dimensions={0}, use_global_device_ids=true | all-gather | bytes 38016 | tf_op jit(solution)/shard_map/all_gather | solution.py:50
  143.6 0.1 copy.65
  143.7 0.4 convolution_bitcast_fusion.11
  144.1 0.4 fusion.7
  144.5 0.1 copy.67
  144.6 0.1 copy.70
  144.7 0.4 convolution_bitcast_fusion.10
  145.2 0.4 fusion.8
  145.5 0.1 copy.72
  145.6 0.1 copy.75
  145.7 0.4 convolution_bitcast_fusion.9
  146.2 0.4 fusion.9
  146.5 0.1 copy.77
  146.6 0.1 copy.80
  146.8 0.4 convolution_bitcast_fusion.8
  147.2 0.4 fusion.10
  147.6 0.1 copy.82
  147.7 0.1 copy.85
  147.8 0.4 convolution_bitcast_fusion.7
  148.2 0.4 fusion.11
  148.6 0.1 copy.87
  148.7 0.1 copy.90
  148.8 0.4 convolution_bitcast_fusion.6
  149.3 0.4 fusion.12
  149.6 0.1 copy.92
  149.7 0.1 copy.95
  149.8 0.4 convolution_bitcast_fusion.5
  150.3 0.4 fusion.13
  150.7 0.1 copy.97
  150.8 0.1 copy.100
  150.9 0.4 convolution_bitcast_fusion.4
  151.3 0.4 fusion.14
  151.7 0.1 copy.102
  151.8 0.1 copy.105
  151.9 0.4 convolution_bitcast_fusion.3
  152.3 0.4 fusion.15
  152.7 0.1 copy.107
  152.8 0.1 copy.110
  152.9 0.4 convolution_bitcast_fusion.2
  153.4 0.4 fusion.16
  153.7 0.1 copy.112
  153.8 0.1 copy.115
  154.0 0.4 convolution_bitcast_fusion.1
  154.4 0.4 fusion.17
  154.8 0.1 copy.117
  154.9 0.1 copy.120
  155.0 0.4 convolution_bitcast_fusion
  155.4 0.4 fusion.18
  155.9 0.1 copy.123
  156.0 0.4 fusion
  156.4 0.7 reshape.15
  157.1 63.8 %all-gather.3.cloned.1.call-done = bf16[96,12288]{1,0:T(8,128)(2,1)} async-done(((bf16[96,384]{1,0:T(8,128)(2,1)}), bf16[96,12288]{1,0:T(8,128)(2,1)}) %all-gather.3.cloned.1.call-update) | async-done | bytes 2359312 | tf_op jit(solution)/shard_map/all_gather | solution.py:54
  220.9 3.3 copy.146
  224.2 8.2 %all-to-all-start = ((bf16[96,8,1536]{2,0,1:T(8,128)(2,1)}), bf16[96,8,1536]{2,0,1:T(8,128)(2,1)}, u32[]{:S(2)}, u32[]{:S(2)}) async-start(bf16[96,8,1536]{2,0,1:T(8,128)(2,1)} %bitcast.119), calls=%async_computation | async-start | bytes 4718592 | tf_op jit(solution)/shard_map/all_to_all | solution.py:55
  232.3 0.6 copy.126
  232.9 100.2 %all_gather.18 = bf16[768,384]{1,0:T(8,128)(2,1)S(1)} all-gather(bf16[96,384]{1,0:T(8,128)(2,1)S(1)} %copy-done.1), channel_id=1, replica_groups=mesh['row'=32,'col'=8] {'col'}, dimensions={0}, use_global_device_ids=true | all-gather | bytes 663552 | tf_op jit(solution)/shard_map/all_gather | solution.py:53
  333.2 4.2 %convolution_multiply_fusion = f32[384,1536]{1,0:T(8,128)} fusion(bf16[768,384]{1,0:T(8,128)(2,1)S(1)} %all_gather.18, bf16[768,1536]{1,0:T(8,128)(2,1)} %bitcast.30), kind=kOutput, calls=%fused_computation | convolution fusion | flops 906559488 | bytes 5308416 | tf_op jit(solution)/shard_map/dot_general | solution.py:28
  (27 shorter events, 0.4 us)
Async XLA Ops:
  7.2 69.3 %copy-start = (f32[384,1536]{1,0:T(8,128)S(1)}, f32[384,1536]{1,0:T(8,128)}, u32[]{:S(2)}) copy-start(f32[384,1536]{1,0:T(8,128)} %param.5) | copy-start | bytes 7077892
  7.2 95.5 %copy-start.2 = (bf16[32,3,384]{2,0,1:T(8,128)(2,1)S(1)}, bf16[32,3,384]{2,0,1:T(8,128)(2,1)}, u32[]{:S(2)}) copy-start(bf16[32,3,384]{2,0,1:T(8,128)(2,1)} %param.3) | copy-start | bytes 221188
  7.2 213.7 %all-gather.3.cloned.1.call-start = ((), (), s32[]{:S(2)}) async-start(), calls=%async_computation.1 | async-start | bytes 2433024 | tf_op jit(solution)/shard_map/all_gather | solution.py:54
  224.2 8.8 %copy-start.1 = (bf16[96,384]{1,0:T(8,128)(2,1)S(1)}, bf16[96,384]{1,0:T(8,128)(2,1)}, u32[]{:S(2)}) copy-start(bf16[96,384]{1,0:T(8,128)(2,1)} %reshape.15) | copy-start | bytes 221188
  224.2 109.0 %all-to-all-start = ((bf16[96,8,1536]{2,0,1:T(8,128)(2,1)}), bf16[96,8,1536]{2,0,1:T(8,128)(2,1)}, u32[]{:S(2)}, u32[]{:S(2)}) async-start(bf16[96,8,1536]{2,0,1:T(8,128)(2,1)} %bitcast.119), calls=%async_computation | async-start | bytes 4718592 | tf_op jit(solution)/shard_map/all_to_all | solution.py:55
Sparse Core Ops, SparseCore 0:
  157.2 63.6 all-gather.2
